TPU v7x, 32 devices: a whole 2x2x4 slice. The times are simulated.
32 devices in a mesh: parts: 2 (over y), leaf: 4 (over z), sub: 4 (over x, core).
Axes of the slice: x: 2, y: 2, z: 4, core: 2. Of those that a mesh axis runs over, the one named last changes fastest.
Arguments:
- points: float32 [6, 65536], P(None, ('parts', 'leaf', 'sub')), parts along dimension 1
- targets: float32 [64, 65536], P(None, ('parts', 'leaf', 'sub')), parts along dimension 1
- leaf_skel: int32 [32, 256], P(('parts', 'leaf', 'sub')), parts along dimension 0, may hold values from 0 to 2047, as said below
- node_keep: int32 [30, 256], P('parts'), parts along dimension 0, may hold values from 0 to 511, as said below
- lengthscales: float32 [12], P('parts'), parts along dimension 0, may hold values from 0.25 to 0.35
- noise_var: float32 [2], P('parts'), parts along dimension 0, may hold values from 0.5 to 1.5
Outputs:
- solution: float32 [64, 65536], P(None, ('parts', 'leaf', 'sub')), parts along dimension 1
- residual: float32 [64, 65536], P(None, ('parts', 'leaf', 'sub')), parts along dimension 1
There are 2 independent parts, one for each index of `parts`. A program takes and returns all parts, laid end to end along the dimension named above; each array names one. Nothing has to cross between parts.
Inputs may be any that keep to these rules, and one draw needn't show every extreme that they name: `leaf_skel`: row t lists 256 distinct positions among the 2048 points of leaf t. `node_keep`: row n lists 256 distinct positions in the concatenation of the skeletons of heap nodes 2n+1 and 2n+2, the first node's 256 points before the second's.
All inputs are finite; a program needn't handle non-finite values.
Results may differ from a plain program's by a relative error of at most 0.0004.
Values sent between devices are 32-bit elements; how exact they have to be, the bound alone decides.
No kernel may reach another device: no remote copies, remote signals or barrier semaphores. Data moves between devices by JAX's collectives and lax.ppermute only.
A program may use at most 128 MiB of HBM per device.

v0:
```python
import jax
import jax.numpy as jnp
from jax import lax
from jax.sharding import PartitionSpec as P

ITERS = 3


def from_partner(shard, axis, stride):
    return lax.ppermute(shard, axis, [(i, i ^ 1 << stride) for i in range(lax.axis_size(axis))])


def kernel(left, right, inverse_scale):
    squared = jnp.zeros((left.shape[1], right.shape[1]), jnp.float32)
    for axis_number in range(left.shape[0]):
        offset = (left[axis_number][:, None] - right[axis_number][None, :]) * inverse_scale[
            axis_number
        ]
        squared = squared + offset * offset
    return jnp.exp(-0.5 * squared)


def product(first, second):
    return jnp.dot(
        first, second, precision=lax.Precision.HIGHEST, preferred_element_type=jnp.float32
    )


def merged(own_part, their_part, on_right):
    return jnp.concatenate(
        [jnp.where(on_right, their_part, own_part), jnp.where(on_right, own_part, their_part)],
        axis=-1,
    )


def climb_up(packed, sibling, on_right, chosen, dims, inverse_scale):
    joined = merged(packed, sibling, on_right)
    joined_coords = joined[:dims]
    parent = jnp.take(joined_coords, chosen, axis=1)
    transfer = kernel(joined_coords, parent, inverse_scale)
    return (parent, product(joined[dims:], transfer), transfer)


def body(points, targets, leaf_skel, node_keep, lengthscales, noise_var):
    dims = points.shape[0]
    leaf_size = points.shape[1]
    skeleton_rank = leaf_skel.shape[1]
    rhs_count = targets.shape[0]
    inverse_scale = 1.0 / lengthscales
    sub_count = lax.axis_size("sub")
    leaf_count = lax.axis_size("leaf")
    sub_levels = sub_count.bit_length() - 1
    levels = sub_levels + leaf_count.bit_length() - 1
    leaf_number = lax.axis_index("leaf") * sub_count + lax.axis_index("sub")
    own_coords = jnp.take(points, leaf_skel[0], axis=1)
    leaf_basis = kernel(points, own_coords, inverse_scale)
    block_width = min(256, leaf_size)
    blocks = leaf_size // block_width

    def pick_rows(tree_level):
        heap_index = (1 << levels - tree_level) - 1 + (leaf_number >> tree_level)
        return lax.dynamic_index_in_dim(node_keep, heap_index, 0, keepdims=False)

    def side_of(tree_level):
        return leaf_number >> tree_level - 1 & 1 == 1

    solution = jnp.zeros_like(targets)
    residual = targets
    direction = targets
    norm_now = lax.psum(jnp.sum(residual * residual, axis=1), ("leaf", "sub"))
    for iteration in range(ITERS):
        node_weight = product(direction, leaf_basis)
        coords = own_coords
        ancestry = []
        for apply_tree_level in range(1, sub_levels + 1):
            on_right = side_of(apply_tree_level)
            packed = jnp.concatenate([coords, node_weight], axis=0)
            sibling = from_partner(packed, "sub", apply_tree_level - 1)
            crossing = kernel(sibling[:dims], coords, inverse_scale)
            sibling_w = sibling[dims:]
            coords, node_weight, transfer = climb_up(
                packed, sibling, on_right, pick_rows(apply_tree_level), dims, inverse_scale
            )
            ancestry.append((transfer, crossing, sibling_w, on_right))
        for apply_tree_level in range(sub_levels + 1, levels + 1):
            on_right = side_of(apply_tree_level)
            packed = jnp.concatenate([coords, node_weight], axis=0)
            sibling = from_partner(packed, "leaf", apply_tree_level - 1 - sub_levels)
            crossing = kernel(sibling[:dims], coords, inverse_scale)
            sibling_w = sibling[dims:]
            coords, node_weight, transfer = climb_up(
                packed, sibling, on_right, pick_rows(apply_tree_level), dims, inverse_scale
            )
            ancestry.append((transfer, crossing, sibling_w, on_right))
        search_vector = jnp.zeros((rhs_count, skeleton_rank), jnp.float32)
        for apply_tree_level in range(levels, 0, -1):
            transfer, crossing, sibling_w, on_right = ancestry[apply_tree_level - 1]
            downward_sweep = product(search_vector, transfer.T)
            own_half = jnp.where(
                on_right, downward_sweep[:, skeleton_rank:], downward_sweep[:, :skeleton_rank]
            )
            search_vector = product(sibling_w, crossing) + own_half
        far_term = product(search_vector, leaf_basis.T)
        values = direction

        def one_block(block_index):
            columns = lax.dynamic_slice_in_dim(points, block_index * block_width, block_width, 1)
            return product(values, kernel(points, columns, inverse_scale))

        pieces = lax.map(one_block, jnp.arange(blocks))
        image = noise_var[0] * direction + (
            jnp.transpose(pieces, (1, 0, 2)).reshape(values.shape[0], leaf_size) + far_term
        )
        curve = lax.psum(jnp.sum(direction * image, axis=1), ("leaf", "sub"))
        step_size = norm_now / curve
        solution = solution + step_size[:, None] * direction
        residual = residual - step_size[:, None] * image
        if iteration + 1 < ITERS:
            norm_next = lax.psum(jnp.sum(residual * residual, axis=1), ("leaf", "sub"))
        if iteration + 1 < ITERS:
            direction = residual + (norm_next / norm_now)[:, None] * direction
            norm_now = norm_next
    return (solution, residual)


def solution(mesh):
    in_specs = (
        P(None, ("parts", "leaf", "sub")),
        P(None, ("parts", "leaf", "sub")),
        P(("parts", "leaf", "sub"), None),
        P("parts", None),
        P("parts"),
        P("parts"),
    )
    out_specs = (P(None, ("parts", "leaf", "sub")), P(None, ("parts", "leaf", "sub")))
    return jax.shard_map(body, mesh=mesh, in_specs=in_specs, out_specs=out_specs, check_vma=False)
```

profile of v0, /device:TPU:0, one launch (start us, length us, event | category | flops | bytes accessed | tf_op | source)
XLA Modules:
  0.0 633.5 jit_solution(1695092716191772870)
XLA Ops:
  4.5 7.0 %convolution_bitcast_fusion = f32[64,256]{1,0:T(8,128)S(1)} fusion(f32[64,2048]{1,0:T(8,128)S(1)} %copy-done.1, f32[]{:T(128)} %bitcast.86, f32[256]{0:T(256)S(1)} %bitcast.707, f32[2048]{0:T(1024)S(1)} %bitcast.534, f32[]{:T(128)} %bitcast.83, f32[256]{0:T(256)S(1)} %bitcast.716, f32[2048]{0:T(1024)S(1)} %bitcast.540, f32[]{:T(128)} %bitcast.80, ...), kind=kOutput, calls=%fused_computation.179 | convolution fusion | flops 415236096 | bytes 645144 | tf_op jit(solution)/shard_map/dot_general | solution.py:24
  12.3 72.7 %while.30 = (s32[]{:T(128)}, f32[8,64,256]{2,1,0:T(8,128)S(1)}, f32[6,2048]{1,0:T(8,128)S(1)}, s32[8]{0:T(128)S(1)}, f32[6]{0:T(128)S(1)}, /*index=5*/f32[64,204...) while((s32[]{:T(128)}, f32[8,64,256]{2,1,0:T(8,128)S(1)}, ...), condition=%wide.region_3.4_spmd, body=%wide.region_2.3_spmd.sunk | while | flops 415236096 | bytes 756071 | solution.py:110
  14.4 6.9 %fusion.1032 = f32[8,64,256]{2,1,0:T(8,128)S(1)} fusion(f32[8,64,256]{2,1,0:T(8,128)S(1)} %get-tuple-element.708, s32[]{:T(128)} %get-tuple-element.707, f32[64,2048]{1,0:T(8,128)S(1)} %get-tuple-element.727, f32[]{:T(128)} %bitcast.420, f32[256]{0:T(256)S(1)} %bitcast.513, f32[2048]{0:T(1024)S(1)} %bitcast.491, f32[]{:T(128)} %bitcast.424, ...), kind=kOutput, calls=%fused_computation.40.clone.1 | convolution fusion | flops 415236096 | bytes 645148 | tf_op jit(solution)/shard_map/while/body/eval_jaxpr/dot_general | solution.py:24
  23.5 6.9 %fusion.1032 = f32[8,64,256]{2,1,0:T(8,128)S(1)} fusion(f32[8,64,256]{2,1,0:T(8,128)S(1)} %get-tuple-element.708, s32[]{:T(128)} %get-tuple-element.707, f32[64,2048]{1,0:T(8,128)S(1)} %get-tuple-element.727, f32[]{:T(128)} %bitcast.420, f32[256]{0:T(256)S(1)} %bitcast.513, f32[2048]{0:T(1024)S(1)} %bitcast.491, f32[]{:T(128)} %bitcast.424, ...), kind=kOutput, calls=%fused_computation.40.clone.1 | convolution fusion | flops 415236096 | bytes 645148 | tf_op jit(solution)/shard_map/while/body/eval_jaxpr/dot_general | solution.py:24
  32.5 6.9 %fusion.1032 = f32[8,64,256]{2,1,0:T(8,128)S(1)} fusion(f32[8,64,256]{2,1,0:T(8,128)S(1)} %get-tuple-element.708, s32[]{:T(128)} %get-tuple-element.707, f32[64,2048]{1,0:T(8,128)S(1)} %get-tuple-element.727, f32[]{:T(128)} %bitcast.420, f32[256]{0:T(256)S(1)} %bitcast.513, f32[2048]{0:T(1024)S(1)} %bitcast.491, f32[]{:T(128)} %bitcast.424, ...), kind=kOutput, calls=%fused_computation.40.clone.1 | convolution fusion | flops 415236096 | bytes 645148 | tf_op jit(solution)/shard_map/while/body/eval_jaxpr/dot_general | solution.py:24
  41.6 6.9 %fusion.1032 = f32[8,64,256]{2,1,0:T(8,128)S(1)} fusion(f32[8,64,256]{2,1,0:T(8,128)S(1)} %get-tuple-element.708, s32[]{:T(128)} %get-tuple-element.707, f32[64,2048]{1,0:T(8,128)S(1)} %get-tuple-element.727, f32[]{:T(128)} %bitcast.420, f32[256]{0:T(256)S(1)} %bitcast.513, f32[2048]{0:T(1024)S(1)} %bitcast.491, f32[]{:T(128)} %bitcast.424, ...), kind=kOutput, calls=%fused_computation.40.clone.1 | convolution fusion | flops 415236096 | bytes 645148 | tf_op jit(solution)/shard_map/while/body/eval_jaxpr/dot_general | solution.py:24
  50.7 6.9 %fusion.1032 = f32[8,64,256]{2,1,0:T(8,128)S(1)} fusion(f32[8,64,256]{2,1,0:T(8,128)S(1)} %get-tuple-element.708, s32[]{:T(128)} %get-tuple-element.707, f32[64,2048]{1,0:T(8,128)S(1)} %get-tuple-element.727, f32[]{:T(128)} %bitcast.420, f32[256]{0:T(256)S(1)} %bitcast.513, f32[2048]{0:T(1024)S(1)} %bitcast.491, f32[]{:T(128)} %bitcast.424, ...), kind=kOutput, calls=%fused_computation.40.clone.1 | convolution fusion | flops 415236096 | bytes 645148 | tf_op jit(solution)/shard_map/while/body/eval_jaxpr/dot_general | solution.py:24
  59.7 6.9 %fusion.1032 = f32[8,64,256]{2,1,0:T(8,128)S(1)} fusion(f32[8,64,256]{2,1,0:T(8,128)S(1)} %get-tuple-element.708, s32[]{:T(128)} %get-tuple-element.707, f32[64,2048]{1,0:T(8,128)S(1)} %get-tuple-element.727, f32[]{:T(128)} %bitcast.420, f32[256]{0:T(256)S(1)} %bitcast.513, f32[2048]{0:T(1024)S(1)} %bitcast.491, f32[]{:T(128)} %bitcast.424, ...), kind=kOutput, calls=%fused_computation.40.clone.1 | convolution fusion | flops 415236096 | bytes 645148 | tf_op jit(solution)/shard_map/while/body/eval_jaxpr/dot_general | solution.py:24
  68.8 6.9 %fusion.1032 = f32[8,64,256]{2,1,0:T(8,128)S(1)} fusion(f32[8,64,256]{2,1,0:T(8,128)S(1)} %get-tuple-element.708, s32[]{:T(128)} %get-tuple-element.707, f32[64,2048]{1,0:T(8,128)S(1)} %get-tuple-element.727, f32[]{:T(128)} %bitcast.420, f32[256]{0:T(256)S(1)} %bitcast.513, f32[2048]{0:T(1024)S(1)} %bitcast.491, f32[]{:T(128)} %bitcast.424, ...), kind=kOutput, calls=%fused_computation.40.clone.1 | convolution fusion | flops 415236096 | bytes 645148 | tf_op jit(solution)/shard_map/while/body/eval_jaxpr/dot_general | solution.py:24
  77.9 6.9 %fusion.1032 = f32[8,64,256]{2,1,0:T(8,128)S(1)} fusion(f32[8,64,256]{2,1,0:T(8,128)S(1)} %get-tuple-element.708, s32[]{:T(128)} %get-tuple-element.707, f32[64,2048]{1,0:T(8,128)S(1)} %get-tuple-element.727, f32[]{:T(128)} %bitcast.420, f32[256]{0:T(256)S(1)} %bitcast.513, f32[2048]{0:T(1024)S(1)} %bitcast.491, f32[]{:T(128)} %bitcast.424, ...), kind=kOutput, calls=%fused_computation.40.clone.1 | convolution fusion | flops 415236096 | bytes 645148 | tf_op jit(solution)/shard_map/while/body/eval_jaxpr/dot_general | solution.py:24
  156.5 8.1 %multiply_reduce_fusion.4 = (f32[64]{0:T(128)S(1)}, f32[64]{0:T(128)S(1)}, f32[64,2048]{1,0:T(8,128)S(1)}) fusion(f32[64,2048]{1,0:T(8,128)S(1)} %get-tuple-element.829, f32[64,2048]{1,0:T(8,128)S(1)} %bitcast.488, f32[64,256]{1,0:T(8,128)S(1)} %convolution_add_fusion.14, f32[]{:T(128)} %bitcast.86, f32[256]{0:T(256)S(1)} %bitcast.709, ...), kind=kOutput, calls=%fused_computation.248 | convolution fusion | flops 416153472 | bytes 1694236 | tf_op jit(solution)/shard_map/dot_general | solution.py:24
  164.5 31.9 %all-reduce = (f32[64]{0:T(128)S(1)}, f32[64]{0:T(128)S(1)}) all-reduce(f32[64]{0:T(128)S(1)} %get-tuple-element.103, f32[64]{0:T(128)S(1)} %get-tuple-element.102), channel_id=1, replica_groups=mesh['parts'=2,'leaf'=4,'sub'=4] {'leaf','sub'}, use_global_device_ids=true, to_apply=%region_1.2 | all-reduce | flops 128 | bytes 1024 | tf_op jit(solution)/shard_map/psum | solution.py:70
  196.7 29.5 %psum.44 = f32[64]{0:T(128)S(1)} all-reduce(f32[64]{0:T(128)S(1)} %multiply_reduce_fusion.3), channel_id=1, replica_groups=mesh['parts'=2,'leaf'=4,'sub'=4] {'leaf','sub'}, use_global_device_ids=true, to_apply=%region_7.9 | all-reduce | flops 64 | bytes 512 | tf_op jit(solution)/shard_map/psum | solution.py:119
  233.3 72.7 %while.31 = (s32[]{:T(128)}, f32[8,64,256]{2,1,0:T(8,128)S(1)}, f32[6,2048]{1,0:T(8,128)S(1)}, s32[8]{0:T(128)S(1)}, f32[6]{0:T(128)S(1)}, /*index=5*/f32[64,204...) while((s32[]{:T(128)}, f32[8,64,256]{2,1,0:T(8,128)S(1)}, ...), condition=%wide.region_9.11_spmd, body=%wide.region_8.10_spmd.sunk | while | flops 415236096 | bytes 756071 | solution.py:110
  244.6 6.9 %fusion.1037 = f32[8,64,256]{2,1,0:T(8,128)S(1)} fusion(f32[8,64,256]{2,1,0:T(8,128)S(1)} %get-tuple-element.753, s32[]{:T(128)} %get-tuple-element.752, f32[64,2048]{1,0:T(8,128)S(1)} %get-tuple-element.772, f32[]{:T(128)} %bitcast.441, f32[256]{0:T(256)S(1)} %bitcast.519, f32[2048]{0:T(1024)S(1)} %bitcast.497, f32[]{:T(128)} %bitcast.445, ...), kind=kOutput, calls=%fused_computation.89.clone.1 | convolution fusion | flops 415236096 | bytes 645148 | tf_op jit(solution)/shard_map/while/body/eval_jaxpr/dot_general | solution.py:24
  262.7 6.9 %fusion.1037 = f32[8,64,256]{2,1,0:T(8,128)S(1)} fusion(f32[8,64,256]{2,1,0:T(8,128)S(1)} %get-tuple-element.753, s32[]{:T(128)} %get-tuple-element.752, f32[64,2048]{1,0:T(8,128)S(1)} %get-tuple-element.772, f32[]{:T(128)} %bitcast.441, f32[256]{0:T(256)S(1)} %bitcast.519, f32[2048]{0:T(1024)S(1)} %bitcast.497, f32[]{:T(128)} %bitcast.445, ...), kind=kOutput, calls=%fused_computation.89.clone.1 | convolution fusion | flops 415236096 | bytes 645148 | tf_op jit(solution)/shard_map/while/body/eval_jaxpr/dot_general | solution.py:24
  280.8 6.9 %fusion.1037 = f32[8,64,256]{2,1,0:T(8,128)S(1)} fusion(f32[8,64,256]{2,1,0:T(8,128)S(1)} %get-tuple-element.753, s32[]{:T(128)} %get-tuple-element.752, f32[64,2048]{1,0:T(8,128)S(1)} %get-tuple-element.772, f32[]{:T(128)} %bitcast.441, f32[256]{0:T(256)S(1)} %bitcast.519, f32[2048]{0:T(1024)S(1)} %bitcast.497, f32[]{:T(128)} %bitcast.445, ...), kind=kOutput, calls=%fused_computation.89.clone.1 | convolution fusion | flops 415236096 | bytes 645148 | tf_op jit(solution)/shard_map/while/body/eval_jaxpr/dot_general | solution.py:24
  298.9 6.9 %fusion.1037 = f32[8,64,256]{2,1,0:T(8,128)S(1)} fusion(f32[8,64,256]{2,1,0:T(8,128)S(1)} %get-tuple-element.753, s32[]{:T(128)} %get-tuple-element.752, f32[64,2048]{1,0:T(8,128)S(1)} %get-tuple-element.772, f32[]{:T(128)} %bitcast.441, f32[256]{0:T(256)S(1)} %bitcast.519, f32[2048]{0:T(1024)S(1)} %bitcast.497, f32[]{:T(128)} %bitcast.445, ...), kind=kOutput, calls=%fused_computation.89.clone.1 | convolution fusion | flops 415236096 | bytes 645148 | tf_op jit(solution)/shard_map/while/body/eval_jaxpr/dot_general | solution.py:24
  376.3 7.9 %multiply_reduce_fusion.2 = (f32[64]{0:T(128)S(1)}, f32[64,2048]{1,0:T(8,128)S(1)}) fusion(f32[64,2048]{1,0:T(8,128)S(1)} %get-tuple-element.832, f32[64,2048]{1,0:T(8,128)S(1)} %bitcast.489, f32[64,256]{1,0:T(8,128)S(1)} %convolution_add_fusion.10, f32[]{:T(128)} %bitcast.86, f32[256]{0:T(256)S(1)} %bitcast.712, f32[2048]{0:T(1024)S(1)} %bitcast.537, ...), kind=kOutput, calls=%fused_computation.215 | convolution fusion | flops 415891392 | bytes 1693980 | tf_op jit(solution)/shard_map/dot_general | solution.py:24
  384.2 29.5 %psum.45 = f32[64]{0:T(128)S(1)} all-reduce(f32[64]{0:T(128)S(1)} %get-tuple-element.463), channel_id=1, replica_groups=mesh['parts'=2,'leaf'=4,'sub'=4] {'leaf','sub'}, use_global_device_ids=true, to_apply=%region_11.13 | all-reduce | flops 64 | bytes 512 | tf_op jit(solution)/shard_map/psum | solution.py:114
  414.3 29.5 %psum.46 = f32[64]{0:T(128)S(1)} all-reduce(f32[64]{0:T(128)S(1)} %get-tuple-element.160), channel_id=1, replica_groups=mesh['parts'=2,'leaf'=4,'sub'=4] {'leaf','sub'}, use_global_device_ids=true, to_apply=%region_13.15 | all-reduce | flops 64 | bytes 512 | tf_op jit(solution)/shard_map/psum | solution.py:119
  451.4 72.2 %while.32 = (s32[]{:T(128)}, f32[8,64,256]{2,1,0:T(8,128)S(1)}, f32[6,2048]{1,0:T(8,128)S(1)}, s32[8]{0:T(128)S(1)}, f32[6]{0:T(128)S(1)}, /*index=5*/f32[64,204...) while((s32[]{:T(128)}, f32[8,64,256]{2,1,0:T(8,128)S(1)}, ...), condition=%wide.region_15.17_spmd, body=%wide.region_14.16_spmd.sunk | while | flops 415236096 | bytes 756071 | solution.py:110
  453.5 6.9 %fusion.1042 = f32[8,64,256]{2,1,0:T(8,128)S(1)} fusion(f32[8,64,256]{2,1,0:T(8,128)S(1)} %get-tuple-element.798, s32[]{:T(128)} %get-tuple-element.797, f32[64,2048]{1,0:T(8,128)S(1)} %get-tuple-element.817, f32[]{:T(128)} %bitcast.462, f32[256]{0:T(256)S(1)} %bitcast.525, f32[2048]{0:T(1024)S(1)} %bitcast.503, f32[]{:T(128)} %bitcast.466, ...), kind=kOutput, calls=%fused_computation.138.clone.1 | convolution fusion | flops 415236096 | bytes 645148 | tf_op jit(solution)/shard_map/while/body/eval_jaxpr/dot_general | solution.py:24
  462.5 6.9 %fusion.1042 = f32[8,64,256]{2,1,0:T(8,128)S(1)} fusion(f32[8,64,256]{2,1,0:T(8,128)S(1)} %get-tuple-element.798, s32[]{:T(128)} %get-tuple-element.797, f32[64,2048]{1,0:T(8,128)S(1)} %get-tuple-element.817, f32[]{:T(128)} %bitcast.462, f32[256]{0:T(256)S(1)} %bitcast.525, f32[2048]{0:T(1024)S(1)} %bitcast.503, f32[]{:T(128)} %bitcast.466, ...), kind=kOutput, calls=%fused_computation.138.clone.1 | convolution fusion | flops 415236096 | bytes 645148 | tf_op jit(solution)/shard_map/while/body/eval_jaxpr/dot_general | solution.py:24
  471.5 6.9 %fusion.1042 = f32[8,64,256]{2,1,0:T(8,128)S(1)} fusion(f32[8,64,256]{2,1,0:T(8,128)S(1)} %get-tuple-element.798, s32[]{:T(128)} %get-tuple-element.797, f32[64,2048]{1,0:T(8,128)S(1)} %get-tuple-element.817, f32[]{:T(128)} %bitcast.462, f32[256]{0:T(256)S(1)} %bitcast.525, f32[2048]{0:T(1024)S(1)} %bitcast.503, f32[]{:T(128)} %bitcast.466, ...), kind=kOutput, calls=%fused_computation.138.clone.1 | convolution fusion | flops 415236096 | bytes 645148 | tf_op jit(solution)/shard_map/while/body/eval_jaxpr/dot_general | solution.py:24
  480.5 6.9 %fusion.1042 = f32[8,64,256]{2,1,0:T(8,128)S(1)} fusion(f32[8,64,256]{2,1,0:T(8,128)S(1)} %get-tuple-element.798, s32[]{:T(128)} %get-tuple-element.797, f32[64,2048]{1,0:T(8,128)S(1)} %get-tuple-element.817, f32[]{:T(128)} %bitcast.462, f32[256]{0:T(256)S(1)} %bitcast.525, f32[2048]{0:T(1024)S(1)} %bitcast.503, f32[]{:T(128)} %bitcast.466, ...), kind=kOutput, calls=%fused_computation.138.clone.1 | convolution fusion | flops 415236096 | bytes 645148 | tf_op jit(solution)/shard_map/while/body/eval_jaxpr/dot_general | solution.py:24
  489.5 6.9 %fusion.1042 = f32[8,64,256]{2,1,0:T(8,128)S(1)} fusion(f32[8,64,256]{2,1,0:T(8,128)S(1)} %get-tuple-element.798, s32[]{:T(128)} %get-tuple-element.797, f32[64,2048]{1,0:T(8,128)S(1)} %get-tuple-element.817, f32[]{:T(128)} %bitcast.462, f32[256]{0:T(256)S(1)} %bitcast.525, f32[2048]{0:T(1024)S(1)} %bitcast.503, f32[]{:T(128)} %bitcast.466, ...), kind=kOutput, calls=%fused_computation.138.clone.1 | convolution fusion | flops 415236096 | bytes 645148 | tf_op jit(solution)/shard_map/while/body/eval_jaxpr/dot_general | solution.py:24
  498.5 6.9 %fusion.1042 = f32[8,64,256]{2,1,0:T(8,128)S(1)} fusion(f32[8,64,256]{2,1,0:T(8,128)S(1)} %get-tuple-element.798, s32[]{:T(128)} %get-tuple-element.797, f32[64,2048]{1,0:T(8,128)S(1)} %get-tuple-element.817, f32[]{:T(128)} %bitcast.462, f32[256]{0:T(256)S(1)} %bitcast.525, f32[2048]{0:T(1024)S(1)} %bitcast.503, f32[]{:T(128)} %bitcast.466, ...), kind=kOutput, calls=%fused_computation.138.clone.1 | convolution fusion | flops 415236096 | bytes 645148 | tf_op jit(solution)/shard_map/while/body/eval_jaxpr/dot_general | solution.py:24
  507.5 6.9 %fusion.1042 = f32[8,64,256]{2,1,0:T(8,128)S(1)} fusion(f32[8,64,256]{2,1,0:T(8,128)S(1)} %get-tuple-element.798, s32[]{:T(128)} %get-tuple-element.797, f32[64,2048]{1,0:T(8,128)S(1)} %get-tuple-element.817, f32[]{:T(128)} %bitcast.462, f32[256]{0:T(256)S(1)} %bitcast.525, f32[2048]{0:T(1024)S(1)} %bitcast.503, f32[]{:T(128)} %bitcast.466, ...), kind=kOutput, calls=%fused_computation.138.clone.1 | convolution fusion | flops 415236096 | bytes 645148 | tf_op jit(solution)/shard_map/while/body/eval_jaxpr/dot_general | solution.py:24
  516.5 6.9 %fusion.1042 = f32[8,64,256]{2,1,0:T(8,128)S(1)} fusion(f32[8,64,256]{2,1,0:T(8,128)S(1)} %get-tuple-element.798, s32[]{:T(128)} %get-tuple-element.797, f32[64,2048]{1,0:T(8,128)S(1)} %get-tuple-element.817, f32[]{:T(128)} %bitcast.462, f32[256]{0:T(256)S(1)} %bitcast.525, f32[2048]{0:T(1024)S(1)} %bitcast.503, f32[]{:T(128)} %bitcast.466, ...), kind=kOutput, calls=%fused_computation.138.clone.1 | convolution fusion | flops 415236096 | bytes 645148 | tf_op jit(solution)/shard_map/while/body/eval_jaxpr/dot_general | solution.py:24
  594.7 7.6 %multiply_reduce_fusion = (f32[64]{0:T(128)S(1)}, f32[64,2048]{1,0:T(8,128)S(1)}) fusion(f32[64,2048]{1,0:T(8,128)S(1)} %get-tuple-element.833, f32[64,2048]{1,0:T(8,128)S(1)} %bitcast.487, f32[64,256]{1,0:T(8,128)S(1)} %convolution_add_fusion.6, f32[]{:T(128)} %bitcast.86, f32[256]{0:T(256)S(1)} %bitcast.715, f32[2048]{0:T(1024)S(1)} %bitcast.539, ...), kind=kOutput, calls=%fused_computation.182 | convolution fusion | flops 415891392 | bytes 1693980 | tf_op jit(solution)/shard_map/dot_general | solution.py:24
  602.3 29.5 %psum.47 = f32[64]{0:T(128)S(1)} all-reduce(f32[64]{0:T(128)S(1)} %get-tuple-element.465), channel_id=1, replica_groups=mesh['parts'=2,'leaf'=4,'sub'=4] {'leaf','sub'}, use_global_device_ids=true, to_apply=%region_17.19 | all-reduce | flops 64 | bytes 512 | tf_op jit(solution)/shard_map/psum | solution.py:114
  (420 shorter events, 294.0 us)
Async XLA Ops:
  2.0 442.4 %copy-start.2 = (f32[1,2048]{1,0:T(1,128)}, f32[1,2048]{1,0:T(1,128)S(1)}, u32[]{:S(2)}) copy-start(f32[1,2048]{1,0:T(1,128)S(1)} %get-tuple-element.388) | copy-start | bytes 24580
  2.0 442.4 %copy-start.4 = (f32[1,2048]{1,0:T(1,128)}, f32[1,2048]{1,0:T(1,128)S(1)}, u32[]{:S(2)}) copy-start(f32[1,2048]{1,0:T(1,128)S(1)} %get-tuple-element.389) | copy-start | bytes 24580
  3.8 440.6 %copy-start.13 = (f32[1,256]{1,0:T(1,128)}, f32[1,256]{1,0:T(1,128)S(1)}, u32[]{:S(2)}) copy-start(f32[1,256]{1,0:T(1,128)S(1)} %get-tuple-element.448) | copy-start | bytes 3076
  3.8 440.6 %copy-start.15 = (f32[1,256]{1,0:T(1,128)}, f32[1,256]{1,0:T(1,128)S(1)}, u32[]{:S(2)}) copy-start(f32[1,256]{1,0:T(1,128)S(1)} %get-tuple-element.449) | copy-start | bytes 3076
  3.8 440.6 %copy-start.17 = (f32[1,256]{1,0:T(1,128)}, f32[1,256]{1,0:T(1,128)S(1)}, u32[]{:S(2)}) copy-start(f32[1,256]{1,0:T(1,128)S(1)} %get-tuple-element.450) | copy-start | bytes 3076
  3.8 440.6 %copy-start.19 = (f32[1,256]{1,0:T(1,128)}, f32[1,256]{1,0:T(1,128)S(1)}, u32[]{:S(2)}) copy-start(f32[1,256]{1,0:T(1,128)S(1)} %get-tuple-element.451) | copy-start | bytes 3076
  3.8 440.6 %copy-start.21 = (f32[1,256]{1,0:T(1,128)}, f32[1,256]{1,0:T(1,128)S(1)}, u32[]{:S(2)}) copy-start(f32[1,256]{1,0:T(1,128)S(1)} %get-tuple-element.452) | copy-start | bytes 3076
  3.8 440.6 %copy-start.23 = (f32[1,256]{1,0:T(1,128)}, f32[1,256]{1,0:T(1,128)S(1)}, u32[]{:S(2)}) copy-start(f32[1,256]{1,0:T(1,128)S(1)} %get-tuple-element.453) | copy-start | bytes 3076
  11.6 74.1 %collective-permute-start = (f32[70,256]{1,0:T(8,128)S(1)}, f32[70,256]{1,0:T(8,128)S(1)}, u32[]{:S(2)}, u32[]{:S(2)}) collective-permute-start(f32[70,256]{1,0:T(8,128)S(1)} %pad_maximum_fusion.2), channel_id=1, source_target_pairs={{0,1},{1,0},{2,3},{3,2},{4,5},{5,4},{6,7},{7,6},{8,9},{9,8},{10,11... | collective-permute-start | bytes 215048 | tf_op jit(solution)/shard_map/ppermute | solution.py:10
  12.1 295.0 %copy-start.8 = (pred[256]{0:T(512)(128)(4,1)}, pred[256]{0:T(512)(128)(4,1)S(1)}, u32[]{:S(2)}) copy-start(pred[256]{0:T(512)(128)(4,1)S(1)} %compare_and_fusion.3) | copy-start | bytes 772
  12.1 305.5 %copy-start.6 = (pred[256]{0:T(512)(128)(4,1)}, pred[256]{0:T(512)(128)(4,1)S(1)}, u32[]{:S(2)}) copy-start(pred[256]{0:T(512)(128)(4,1)S(1)} %compare_and_fusion.2) | copy-start | bytes 772
  91.5 5.5 collective-permute-start.1
  102.7 4.4 collective-permute-start.2
  112.8 5.3 collective-permute-start.3
  233.2 72.9 %collective-permute-start.4 = (f32[70,256]{1,0:T(8,128)S(1)}, f32[70,256]{1,0:T(8,128)S(1)}, u32[]{:S(2)}, u32[]{:S(2)}) collective-permute-start(f32[70,256]{1,0:T(8,128)S(1)} %pad_maximum_fusion.1), channel_id=1, source_target_pairs={{0,1},{1,0},{2,3},{3,2},{4,5},{5,4},{6,7},{7,6},{8,9},{9,8},{10,11... | collective-permute-start | bytes 215048 | tf_op jit(solution)/shard_map/ppermute | solution.py:10
  311.8 4.7 collective-permute-start.5
  322.3 4.4 collective-permute-start.6
  332.5 5.5 collective-permute-start.7
  451.3 72.4 %collective-permute-start.8 = (f32[70,256]{1,0:T(8,128)S(1)}, f32[70,256]{1,0:T(8,128)S(1)}, u32[]{:S(2)}, u32[]{:S(2)}) collective-permute-start(f32[70,256]{1,0:T(8,128)S(1)} %pad_maximum_fusion), channel_id=1, source_target_pairs={{0,1},{1,0},{2,3},{3,2},{4,5},{5,4},{6,7},{7,6},{8,9},{9,8},{10,11... | collective-permute-start | bytes 215048 | tf_op jit(solution)/shard_map/ppermute | solution.py:10
  529.5 5.8 copy-start.7
  529.5 4.7 collective-permute-start.9
  540.1 4.4 collective-permute-start.10
  550.3 5.5 collective-permute-start.11
  585.2 5.0 copy-start.14
  585.2 5.0 copy-start.16
  585.2 5.0 copy-start.18
  585.2 5.0 copy-start.20
  585.2 5.0 copy-start.22
  585.2 5.0 copy-start.24
  585.2 5.0 copy-start.25
  594.6 37.2 %copy-start.51 = (f32[64]{0:T(128)S(1)}, f32[64]{0:T(128)}, u32[]{:S(2)}) copy-start(f32[64]{0:T(128)} %copy-done.50) | copy-start | bytes 772
  594.6 37.2 %copy-start.12 = (f32[64]{0:T(128)S(1)}, f32[64]{0:T(128)}, u32[]{:S(2)}) copy-start(f32[64]{0:T(128)} %copy-done.11) | copy-start | bytes 772
  (32 other events, 133.6 us)
where the time goes:
time: 643 us; the launch traced here: 633 us
  matrix products  362 us (56%)
  blocking collectives  150 us (23%)
  local copies, waits for them, and re-layouts  53.5 us (8%)
  waiting for transfers between devices  35.5 us (6%)
  loops' own time  17.4 us (3%)
  starting transfers between devices  8.43 us (1%)
    dot_general x63, matrix products, product(): jnp.dot(first, second, precision=lax.Precision.HIGHEST, preferred_element...  362 us
    psum x2, blocking collectives, body(): curve = lax.psum(jnp.sum(direction * image, axis=1), ('leaf', 'sub'))  59 us
    psum x2, blocking collectives, body(): norm_next = lax.psum(jnp.sum(residual * residual, axis=1), ('leaf', 'sub'))  59 us
    ppermute x12, waiting for transfers between devices, from_partner(): lax.ppermute(shard, axis, [(i, i ^ 1 << stride) for i in range(lax.axis_s...  35.5 us
    psum x1, blocking collectives, body(): norm_now = lax.psum(jnp.sum(residual * residual, axis=1), ('leaf', 'sub'))  31.9 us
    another operation x3, loops' own time, body(): pieces = lax.map(one_block, jnp.arange(blocks))  17.4 us
    slice x25, local copies, waits for them, and re-layouts, kernel(): inverse_scale[axis_number]  16.8 us
    dynamic_slice x24, local copies, waits for them, and re-layouts, body(): pieces = lax.map(one_block, jnp.arange(blocks))  15.3 us
  transfers between devices with their start and end apart: 12, of which 9 were waited for; matrix products, arithmetic and copies ran while one was open for 32% of the time, Pallas kernels for 0%

commit v1 on v0

--- a/solution.py
+++ b/solution.py
@@ -116,7 +116,7 @@
         solution = solution + step_size[:, None] * direction
         residual = residual - step_size[:, None] * image
         if iteration + 1 < ITERS:
-            norm_next = lax.psum(jnp.sum(residual * residual, axis=1), ("leaf", "sub"))
+            norm_next = lax.psum(lax.psum(jnp.sum(residual * residual, axis=1), "sub"), "leaf")
         if iteration + 1 < ITERS:
             direction = residual + (norm_next / norm_now)[:, None] * direction
             norm_now = norm_next

time: 643 us -> 611 us (0.950)
  blocking collectives: 150 us -> 120 us
  waiting for transfers between devices: 35.5 us -> 28.1 us
  starting transfers between devices: 8.43 us -> 15.4 us
    psum x2 -> x4, blocking collectives: 59 us -> 28.2 us  [the longest x2 16.7 us: body(): lax.psum(lax.psum(jnp.sum(residual * residual, axis=1), 'sub'), 'leaf')]
    ppermute x12, waiting for transfers between devices: 35.5 us -> 28.1 us  [from_partner(): lax.ppermute(shard, axis, [(i, i ^ 1 << stride) for i in range(lax.axis_s...]
    ppermute x12, starting transfers between devices: 8.43 us -> 15.4 us  [from_partner(): lax.ppermute(shard, axis, [(i, i ^ 1 << stride) for i in range(lax.axis_s...]
  transfers between devices with their start and end apart: 12 -> 12, of which waited for: 9 -> 9; matrix products, arithmetic and copies ran while one was open for 32% -> 34% of each run, Pallas kernels for 0% -> 0%
where the time goes in v1:
time: 611 us; the launch traced here: 602 us
  matrix products  364 us (60%)
  blocking collectives  120 us (20%)
  local copies, waits for them, and re-layouts  52.2 us (9%)
  waiting for transfers between devices  28.1 us (5%)
  starting transfers between devices  15.4 us (3%)
  loops' own time  15.4 us (3%)
    dot_general x63, matrix products, product(): jnp.dot(first, second, precision=lax.Precision.HIGHEST, preferred_element...  364 us
    psum x2, blocking collectives, body(): curve = lax.psum(jnp.sum(direction * image, axis=1), ('leaf', 'sub'))  59.6 us
    psum x1, blocking collectives, body(): norm_now = lax.psum(jnp.sum(residual * residual, axis=1), ('leaf', 'sub'))  31.9 us
    ppermute x12, waiting for transfers between devices, from_partner(): lax.ppermute(shard, axis, [(i, i ^ 1 << stride) for i in range(lax.axis_s...  28.1 us
    psum x2, blocking collectives, body(): lax.psum(lax.psum(jnp.sum(residual * residual, axis=1), 'sub'), 'leaf')  16.7 us
    slice x25, local copies, waits for them, and re-layouts, kernel(): inverse_scale[axis_number]  16.6 us
    another operation x3, loops' own time, body(): pieces = lax.map(one_block, jnp.arange(blocks))  15.4 us
    ppermute x12, starting transfers between devices, from_partner(): lax.ppermute(shard, axis, [(i, i ^ 1 << stride) for i in range(lax.axis_s...  15.4 us
  transfers between devices with their start and end apart: 12, of which 9 were waited for; matrix products, arithmetic and copies ran while one was open for 34% of the time, Pallas kernels for 0%

profile of v1, /device:TPU:0, one launch (start us, length us, event | category | flops | bytes accessed | tf_op | source)
XLA Modules:
  0.0 601.9 jit_solution(18124605497020648596)
XLA Ops:
  4.5 7.0 %convolution_bitcast_fusion = f32[64,256]{1,0:T(8,128)S(1)} fusion(f32[64,2048]{1,0:T(8,128)S(1)} %copy-done.1, f32[]{:T(128)} %bitcast.86, f32[256]{0:T(256)S(1)} %bitcast.707, f32[2048]{0:T(1024)S(1)} %bitcast.534, f32[]{:T(128)} %bitcast.83, f32[256]{0:T(256)S(1)} %bitcast.716, f32[2048]{0:T(1024)S(1)} %bitcast.540, f32[]{:T(128)} %bitcast.80, ...), kind=kOutput, calls=%fused_computation.179 | convolution fusion | flops 415236096 | bytes 645144 | tf_op jit(solution)/shard_map/dot_general | solution.py:24
  12.3 72.0 %while.30 = (s32[]{:T(128)}, f32[8,64,256]{2,1,0:T(8,128)S(1)}, f32[6,2048]{1,0:T(8,128)S(1)}, s32[8]{0:T(128)S(1)}, f32[6]{0:T(128)S(1)}, /*index=5*/f32[64,204...) while((s32[]{:T(128)}, f32[8,64,256]{2,1,0:T(8,128)S(1)}, ...), condition=%wide.region_3.4_spmd, body=%wide.region_2.3_spmd.sunk | while | flops 415236096 | bytes 756071 | solution.py:110
  14.2 7.0 %fusion.1032 = f32[8,64,256]{2,1,0:T(8,128)S(1)} fusion(f32[8,64,256]{2,1,0:T(8,128)S(1)} %get-tuple-element.708, s32[]{:T(128)} %get-tuple-element.707, f32[64,2048]{1,0:T(8,128)S(1)} %get-tuple-element.727, f32[]{:T(128)} %bitcast.420, f32[256]{0:T(256)S(1)} %bitcast.513, f32[2048]{0:T(1024)S(1)} %bitcast.491, f32[]{:T(128)} %bitcast.424, ...), kind=kOutput, calls=%fused_computation.40.clone.1 | convolution fusion | flops 415236096 | bytes 645148 | tf_op jit(solution)/shard_map/while/body/eval_jaxpr/dot_general | solution.py:24
  23.2 7.0 %fusion.1032 = f32[8,64,256]{2,1,0:T(8,128)S(1)} fusion(f32[8,64,256]{2,1,0:T(8,128)S(1)} %get-tuple-element.708, s32[]{:T(128)} %get-tuple-element.707, f32[64,2048]{1,0:T(8,128)S(1)} %get-tuple-element.727, f32[]{:T(128)} %bitcast.420, f32[256]{0:T(256)S(1)} %bitcast.513, f32[2048]{0:T(1024)S(1)} %bitcast.491, f32[]{:T(128)} %bitcast.424, ...), kind=kOutput, calls=%fused_computation.40.clone.1 | convolution fusion | flops 415236096 | bytes 645148 | tf_op jit(solution)/shard_map/while/body/eval_jaxpr/dot_general | solution.py:24
  32.2 7.0 %fusion.1032 = f32[8,64,256]{2,1,0:T(8,128)S(1)} fusion(f32[8,64,256]{2,1,0:T(8,128)S(1)} %get-tuple-element.708, s32[]{:T(128)} %get-tuple-element.707, f32[64,2048]{1,0:T(8,128)S(1)} %get-tuple-element.727, f32[]{:T(128)} %bitcast.420, f32[256]{0:T(256)S(1)} %bitcast.513, f32[2048]{0:T(1024)S(1)} %bitcast.491, f32[]{:T(128)} %bitcast.424, ...), kind=kOutput, calls=%fused_computation.40.clone.1 | convolution fusion | flops 415236096 | bytes 645148 | tf_op jit(solution)/shard_map/while/body/eval_jaxpr/dot_general | solution.py:24
  41.1 7.0 %fusion.1032 = f32[8,64,256]{2,1,0:T(8,128)S(1)} fusion(f32[8,64,256]{2,1,0:T(8,128)S(1)} %get-tuple-element.708, s32[]{:T(128)} %get-tuple-element.707, f32[64,2048]{1,0:T(8,128)S(1)} %get-tuple-element.727, f32[]{:T(128)} %bitcast.420, f32[256]{0:T(256)S(1)} %bitcast.513, f32[2048]{0:T(1024)S(1)} %bitcast.491, f32[]{:T(128)} %bitcast.424, ...), kind=kOutput, calls=%fused_computation.40.clone.1 | convolution fusion | flops 415236096 | bytes 645148 | tf_op jit(solution)/shard_map/while/body/eval_jaxpr/dot_general | solution.py:24
  50.1 7.0 %fusion.1032 = f32[8,64,256]{2,1,0:T(8,128)S(1)} fusion(f32[8,64,256]{2,1,0:T(8,128)S(1)} %get-tuple-element.708, s32[]{:T(128)} %get-tuple-element.707, f32[64,2048]{1,0:T(8,128)S(1)} %get-tuple-element.727, f32[]{:T(128)} %bitcast.420, f32[256]{0:T(256)S(1)} %bitcast.513, f32[2048]{0:T(1024)S(1)} %bitcast.491, f32[]{:T(128)} %bitcast.424, ...), kind=kOutput, calls=%fused_computation.40.clone.1 | convolution fusion | flops 415236096 | bytes 645148 | tf_op jit(solution)/shard_map/while/body/eval_jaxpr/dot_general | solution.py:24
  59.1 7.0 %fusion.1032 = f32[8,64,256]{2,1,0:T(8,128)S(1)} fusion(f32[8,64,256]{2,1,0:T(8,128)S(1)} %get-tuple-element.708, s32[]{:T(128)} %get-tuple-element.707, f32[64,2048]{1,0:T(8,128)S(1)} %get-tuple-element.727, f32[]{:T(128)} %bitcast.420, f32[256]{0:T(256)S(1)} %bitcast.513, f32[2048]{0:T(1024)S(1)} %bitcast.491, f32[]{:T(128)} %bitcast.424, ...), kind=kOutput, calls=%fused_computation.40.clone.1 | convolution fusion | flops 415236096 | bytes 645148 | tf_op jit(solution)/shard_map/while/body/eval_jaxpr/dot_general | solution.py:24
  68.0 7.0 %fusion.1032 = f32[8,64,256]{2,1,0:T(8,128)S(1)} fusion(f32[8,64,256]{2,1,0:T(8,128)S(1)} %get-tuple-element.708, s32[]{:T(128)} %get-tuple-element.707, f32[64,2048]{1,0:T(8,128)S(1)} %get-tuple-element.727, f32[]{:T(128)} %bitcast.420, f32[256]{0:T(256)S(1)} %bitcast.513, f32[2048]{0:T(1024)S(1)} %bitcast.491, f32[]{:T(128)} %bitcast.424, ...), kind=kOutput, calls=%fused_computation.40.clone.1 | convolution fusion | flops 415236096 | bytes 645148 | tf_op jit(solution)/shard_map/while/body/eval_jaxpr/dot_general | solution.py:24
  77.0 7.0 %fusion.1032 = f32[8,64,256]{2,1,0:T(8,128)S(1)} fusion(f32[8,64,256]{2,1,0:T(8,128)S(1)} %get-tuple-element.708, s32[]{:T(128)} %get-tuple-element.707, f32[64,2048]{1,0:T(8,128)S(1)} %get-tuple-element.727, f32[]{:T(128)} %bitcast.420, f32[256]{0:T(256)S(1)} %bitcast.513, f32[2048]{0:T(1024)S(1)} %bitcast.491, f32[]{:T(128)} %bitcast.424, ...), kind=kOutput, calls=%fused_computation.40.clone.1 | convolution fusion | flops 415236096 | bytes 645148 | tf_op jit(solution)/shard_map/while/body/eval_jaxpr/dot_general | solution.py:24
  155.8 8.1 %multiply_reduce_fusion.4 = (f32[64]{0:T(128)S(1)}, f32[64]{0:T(128)S(1)}, f32[64,2048]{1,0:T(8,128)S(1)}) fusion(f32[64,2048]{1,0:T(8,128)S(1)} %get-tuple-element.829, f32[64,2048]{1,0:T(8,128)S(1)} %bitcast.488, f32[64,256]{1,0:T(8,128)S(1)} %convolution_add_fusion.14, f32[]{:T(128)} %bitcast.86, f32[256]{0:T(256)S(1)} %bitcast.709, ...), kind=kOutput, calls=%fused_computation.248 | convolution fusion | flops 416153472 | bytes 1694236 | tf_op jit(solution)/shard_map/dot_general | solution.py:24
  163.8 31.9 %all-reduce = (f32[64]{0:T(128)S(1)}, f32[64]{0:T(128)S(1)}) all-reduce(f32[64]{0:T(128)S(1)} %get-tuple-element.103, f32[64]{0:T(128)S(1)} %get-tuple-element.102), channel_id=1, replica_groups=mesh['parts'=2,'leaf'=4,'sub'=4] {'leaf','sub'}, use_global_device_ids=true, to_apply=%region_1.2 | all-reduce | flops 128 | bytes 1024 | tf_op jit(solution)/shard_map/psum | solution.py:70
  201.8 8.4 %psum.59 = f32[64]{0:T(128)S(1)} all-reduce(f32[64]{0:T(128)S(1)} %psum.58), channel_id=1, replica_groups=mesh['parts'=2,'leaf'=4,'sub'=4] {'leaf'}, use_global_device_ids=true, to_apply=%region_8.10 | all-reduce | flops 64 | bytes 512 | tf_op jit(solution)/shard_map/psum | solution.py:119
  217.3 71.9 %while.31 = (s32[]{:T(128)}, f32[8,64,256]{2,1,0:T(8,128)S(1)}, f32[6,2048]{1,0:T(8,128)S(1)}, s32[8]{0:T(128)S(1)}, f32[6]{0:T(128)S(1)}, /*index=5*/f32[64,204...) while((s32[]{:T(128)}, f32[8,64,256]{2,1,0:T(8,128)S(1)}, ...), condition=%wide.region_10.12_spmd, body=%wide.region_9.11_spmd.sunk | while | flops 415236096 | bytes 756071 | solution.py:110
  219.2 7.0 %fusion.1037 = f32[8,64,256]{2,1,0:T(8,128)S(1)} fusion(f32[8,64,256]{2,1,0:T(8,128)S(1)} %get-tuple-element.753, s32[]{:T(128)} %get-tuple-element.752, f32[64,2048]{1,0:T(8,128)S(1)} %get-tuple-element.772, f32[]{:T(128)} %bitcast.441, f32[256]{0:T(256)S(1)} %bitcast.519, f32[2048]{0:T(1024)S(1)} %bitcast.497, f32[]{:T(128)} %bitcast.445, ...), kind=kOutput, calls=%fused_computation.89.clone.1 | convolution fusion | flops 415236096 | bytes 645148 | tf_op jit(solution)/shard_map/while/body/eval_jaxpr/dot_general | solution.py:24
  228.2 7.0 %fusion.1037 = f32[8,64,256]{2,1,0:T(8,128)S(1)} fusion(f32[8,64,256]{2,1,0:T(8,128)S(1)} %get-tuple-element.753, s32[]{:T(128)} %get-tuple-element.752, f32[64,2048]{1,0:T(8,128)S(1)} %get-tuple-element.772, f32[]{:T(128)} %bitcast.441, f32[256]{0:T(256)S(1)} %bitcast.519, f32[2048]{0:T(1024)S(1)} %bitcast.497, f32[]{:T(128)} %bitcast.445, ...), kind=kOutput, calls=%fused_computation.89.clone.1 | convolution fusion | flops 415236096 | bytes 645148 | tf_op jit(solution)/shard_map/while/body/eval_jaxpr/dot_general | solution.py:24
  237.2 7.0 %fusion.1037 = f32[8,64,256]{2,1,0:T(8,128)S(1)} fusion(f32[8,64,256]{2,1,0:T(8,128)S(1)} %get-tuple-element.753, s32[]{:T(128)} %get-tuple-element.752, f32[64,2048]{1,0:T(8,128)S(1)} %get-tuple-element.772, f32[]{:T(128)} %bitcast.441, f32[256]{0:T(256)S(1)} %bitcast.519, f32[2048]{0:T(1024)S(1)} %bitcast.497, f32[]{:T(128)} %bitcast.445, ...), kind=kOutput, calls=%fused_computation.89.clone.1 | convolution fusion | flops 415236096 | bytes 645148 | tf_op jit(solution)/shard_map/while/body/eval_jaxpr/dot_general | solution.py:24
  246.1 7.0 %fusion.1037 = f32[8,64,256]{2,1,0:T(8,128)S(1)} fusion(f32[8,64,256]{2,1,0:T(8,128)S(1)} %get-tuple-element.753, s32[]{:T(128)} %get-tuple-element.752, f32[64,2048]{1,0:T(8,128)S(1)} %get-tuple-element.772, f32[]{:T(128)} %bitcast.441, f32[256]{0:T(256)S(1)} %bitcast.519, f32[2048]{0:T(1024)S(1)} %bitcast.497, f32[]{:T(128)} %bitcast.445, ...), kind=kOutput, calls=%fused_computation.89.clone.1 | convolution fusion | flops 415236096 | bytes 645148 | tf_op jit(solution)/shard_map/while/body/eval_jaxpr/dot_general | solution.py:24
  255.1 7.0 %fusion.1037 = f32[8,64,256]{2,1,0:T(8,128)S(1)} fusion(f32[8,64,256]{2,1,0:T(8,128)S(1)} %get-tuple-element.753, s32[]{:T(128)} %get-tuple-element.752, f32[64,2048]{1,0:T(8,128)S(1)} %get-tuple-element.772, f32[]{:T(128)} %bitcast.441, f32[256]{0:T(256)S(1)} %bitcast.519, f32[2048]{0:T(1024)S(1)} %bitcast.497, f32[]{:T(128)} %bitcast.445, ...), kind=kOutput, calls=%fused_computation.89.clone.1 | convolution fusion | flops 415236096 | bytes 645148 | tf_op jit(solution)/shard_map/while/body/eval_jaxpr/dot_general | solution.py:24
  264.1 7.0 %fusion.1037 = f32[8,64,256]{2,1,0:T(8,128)S(1)} fusion(f32[8,64,256]{2,1,0:T(8,128)S(1)} %get-tuple-element.753, s32[]{:T(128)} %get-tuple-element.752, f32[64,2048]{1,0:T(8,128)S(1)} %get-tuple-element.772, f32[]{:T(128)} %bitcast.441, f32[256]{0:T(256)S(1)} %bitcast.519, f32[2048]{0:T(1024)S(1)} %bitcast.497, f32[]{:T(128)} %bitcast.445, ...), kind=kOutput, calls=%fused_computation.89.clone.1 | convolution fusion | flops 415236096 | bytes 645148 | tf_op jit(solution)/shard_map/while/body/eval_jaxpr/dot_general | solution.py:24
  273.0 7.0 %fusion.1037 = f32[8,64,256]{2,1,0:T(8,128)S(1)} fusion(f32[8,64,256]{2,1,0:T(8,128)S(1)} %get-tuple-element.753, s32[]{:T(128)} %get-tuple-element.752, f32[64,2048]{1,0:T(8,128)S(1)} %get-tuple-element.772, f32[]{:T(128)} %bitcast.441, f32[256]{0:T(256)S(1)} %bitcast.519, f32[2048]{0:T(1024)S(1)} %bitcast.497, f32[]{:T(128)} %bitcast.445, ...), kind=kOutput, calls=%fused_computation.89.clone.1 | convolution fusion | flops 415236096 | bytes 645148 | tf_op jit(solution)/shard_map/while/body/eval_jaxpr/dot_general | solution.py:24
  282.0 7.0 %fusion.1037 = f32[8,64,256]{2,1,0:T(8,128)S(1)} fusion(f32[8,64,256]{2,1,0:T(8,128)S(1)} %get-tuple-element.753, s32[]{:T(128)} %get-tuple-element.752, f32[64,2048]{1,0:T(8,128)S(1)} %get-tuple-element.772, f32[]{:T(128)} %bitcast.441, f32[256]{0:T(256)S(1)} %bitcast.519, f32[2048]{0:T(1024)S(1)} %bitcast.497, f32[]{:T(128)} %bitcast.445, ...), kind=kOutput, calls=%fused_computation.89.clone.1 | convolution fusion | flops 415236096 | bytes 645148 | tf_op jit(solution)/shard_map/while/body/eval_jaxpr/dot_general | solution.py:24
  359.4 7.9 %multiply_reduce_fusion.2 = (f32[64]{0:T(128)S(1)}, f32[64,2048]{1,0:T(8,128)S(1)}) fusion(f32[64,2048]{1,0:T(8,128)S(1)} %get-tuple-element.832, f32[64,2048]{1,0:T(8,128)S(1)} %bitcast.489, f32[64,256]{1,0:T(8,128)S(1)} %convolution_add_fusion.10, f32[]{:T(128)} %bitcast.86, f32[256]{0:T(256)S(1)} %bitcast.712, f32[2048]{0:T(1024)S(1)} %bitcast.537, ...), kind=kOutput, calls=%fused_computation.215 | convolution fusion | flops 415891392 | bytes 1693980 | tf_op jit(solution)/shard_map/dot_general | solution.py:24
  367.2 29.5 %psum.60 = f32[64]{0:T(128)S(1)} all-reduce(f32[64]{0:T(128)S(1)} %get-tuple-element.463), channel_id=1, replica_groups=mesh['parts'=2,'leaf'=4,'sub'=4] {'leaf','sub'}, use_global_device_ids=true, to_apply=%region_12.14 | all-reduce | flops 64 | bytes 512 | tf_op jit(solution)/shard_map/psum | solution.py:114
  403.0 8.4 %psum.62 = f32[64]{0:T(128)S(1)} all-reduce(f32[64]{0:T(128)S(1)} %psum.61), channel_id=1, replica_groups=mesh['parts'=2,'leaf'=4,'sub'=4] {'leaf'}, use_global_device_ids=true, to_apply=%region_15.17 | all-reduce | flops 64 | bytes 512 | tf_op jit(solution)/shard_map/psum | solution.py:119
  419.1 72.5 %while.32 = (s32[]{:T(128)}, f32[8,64,256]{2,1,0:T(8,128)S(1)}, f32[6,2048]{1,0:T(8,128)S(1)}, s32[8]{0:T(128)S(1)}, f32[6]{0:T(128)S(1)}, /*index=5*/f32[64,204...) while((s32[]{:T(128)}, f32[8,64,256]{2,1,0:T(8,128)S(1)}, ...), condition=%wide.region_17.19_spmd, body=%wide.region_16.18_spmd.sunk | while | flops 415236096 | bytes 756071 | solution.py:110
  421.2 7.0 %fusion.1042 = f32[8,64,256]{2,1,0:T(8,128)S(1)} fusion(f32[8,64,256]{2,1,0:T(8,128)S(1)} %get-tuple-element.798, s32[]{:T(128)} %get-tuple-element.797, f32[64,2048]{1,0:T(8,128)S(1)} %get-tuple-element.817, f32[]{:T(128)} %bitcast.462, f32[256]{0:T(256)S(1)} %bitcast.525, f32[2048]{0:T(1024)S(1)} %bitcast.503, f32[]{:T(128)} %bitcast.466, ...), kind=kOutput, calls=%fused_computation.138.clone.1 | convolution fusion | flops 415236096 | bytes 645148 | tf_op jit(solution)/shard_map/while/body/eval_jaxpr/dot_general | solution.py:24
  439.2 7.0 %fusion.1042 = f32[8,64,256]{2,1,0:T(8,128)S(1)} fusion(f32[8,64,256]{2,1,0:T(8,128)S(1)} %get-tuple-element.798, s32[]{:T(128)} %get-tuple-element.797, f32[64,2048]{1,0:T(8,128)S(1)} %get-tuple-element.817, f32[]{:T(128)} %bitcast.462, f32[256]{0:T(256)S(1)} %bitcast.525, f32[2048]{0:T(1024)S(1)} %bitcast.503, f32[]{:T(128)} %bitcast.466, ...), kind=kOutput, calls=%fused_computation.138.clone.1 | convolution fusion | flops 415236096 | bytes 645148 | tf_op jit(solution)/shard_map/while/body/eval_jaxpr/dot_general | solution.py:24
  448.3 7.0 %fusion.1042 = f32[8,64,256]{2,1,0:T(8,128)S(1)} fusion(f32[8,64,256]{2,1,0:T(8,128)S(1)} %get-tuple-element.798, s32[]{:T(128)} %get-tuple-element.797, f32[64,2048]{1,0:T(8,128)S(1)} %get-tuple-element.817, f32[]{:T(128)} %bitcast.462, f32[256]{0:T(256)S(1)} %bitcast.525, f32[2048]{0:T(1024)S(1)} %bitcast.503, f32[]{:T(128)} %bitcast.466, ...), kind=kOutput, calls=%fused_computation.138.clone.1 | convolution fusion | flops 415236096 | bytes 645148 | tf_op jit(solution)/shard_map/while/body/eval_jaxpr/dot_general | solution.py:24
  475.4 7.0 %fusion.1042 = f32[8,64,256]{2,1,0:T(8,128)S(1)} fusion(f32[8,64,256]{2,1,0:T(8,128)S(1)} %get-tuple-element.798, s32[]{:T(128)} %get-tuple-element.797, f32[64,2048]{1,0:T(8,128)S(1)} %get-tuple-element.817, f32[]{:T(128)} %bitcast.462, f32[256]{0:T(256)S(1)} %bitcast.525, f32[2048]{0:T(1024)S(1)} %bitcast.503, f32[]{:T(128)} %bitcast.466, ...), kind=kOutput, calls=%fused_computation.138.clone.1 | convolution fusion | flops 415236096 | bytes 645148 | tf_op jit(solution)/shard_map/while/body/eval_jaxpr/dot_general | solution.py:24
  562.4 7.7 %multiply_reduce_fusion = (f32[64]{0:T(128)S(1)}, f32[64,2048]{1,0:T(8,128)S(1)}) fusion(f32[64,2048]{1,0:T(8,128)S(1)} %get-tuple-element.833, f32[64,2048]{1,0:T(8,128)S(1)} %bitcast.487, f32[64,256]{1,0:T(8,128)S(1)} %convolution_add_fusion.6, f32[]{:T(128)} %bitcast.86, f32[256]{0:T(256)S(1)} %bitcast.715, f32[2048]{0:T(1024)S(1)} %bitcast.539, ...), kind=kOutput, calls=%fused_computation.182 | convolution fusion | flops 415891392 | bytes 1693980 | tf_op jit(solution)/shard_map/dot_general | solution.py:24
  570.1 30.1 %psum.63 = f32[64]{0:T(128)S(1)} all-reduce(f32[64]{0:T(128)S(1)} %get-tuple-element.465), channel_id=1, replica_groups=mesh['parts'=2,'leaf'=4,'sub'=4] {'leaf','sub'}, use_global_device_ids=true, to_apply=%region_19.21 | all-reduce | flops 64 | bytes 512 | tf_op jit(solution)/shard_map/psum | solution.py:114
  (422 shorter events, 304.3 us)
Async XLA Ops:
  2.0 410.1 %copy-start.2 = (f32[1,2048]{1,0:T(1,128)}, f32[1,2048]{1,0:T(1,128)S(1)}, u32[]{:S(2)}) copy-start(f32[1,2048]{1,0:T(1,128)S(1)} %get-tuple-element.388) | copy-start | bytes 24580
  2.0 410.1 %copy-start.4 = (f32[1,2048]{1,0:T(1,128)}, f32[1,2048]{1,0:T(1,128)S(1)}, u32[]{:S(2)}) copy-start(f32[1,2048]{1,0:T(1,128)S(1)} %get-tuple-element.389) | copy-start | bytes 24580
  3.8 408.3 %copy-start.13 = (f32[1,256]{1,0:T(1,128)}, f32[1,256]{1,0:T(1,128)S(1)}, u32[]{:S(2)}) copy-start(f32[1,256]{1,0:T(1,128)S(1)} %get-tuple-element.448) | copy-start | bytes 3076
  3.8 408.3 %copy-start.15 = (f32[1,256]{1,0:T(1,128)}, f32[1,256]{1,0:T(1,128)S(1)}, u32[]{:S(2)}) copy-start(f32[1,256]{1,0:T(1,128)S(1)} %get-tuple-element.449) | copy-start | bytes 3076
  3.8 408.3 %copy-start.17 = (f32[1,256]{1,0:T(1,128)}, f32[1,256]{1,0:T(1,128)S(1)}, u32[]{:S(2)}) copy-start(f32[1,256]{1,0:T(1,128)S(1)} %get-tuple-element.450) | copy-start | bytes 3076
  3.8 408.3 %copy-start.19 = (f32[1,256]{1,0:T(1,128)}, f32[1,256]{1,0:T(1,128)S(1)}, u32[]{:S(2)}) copy-start(f32[1,256]{1,0:T(1,128)S(1)} %get-tuple-element.451) | copy-start | bytes 3076
  3.8 408.3 %copy-start.21 = (f32[1,256]{1,0:T(1,128)}, f32[1,256]{1,0:T(1,128)S(1)}, u32[]{:S(2)}) copy-start(f32[1,256]{1,0:T(1,128)S(1)} %get-tuple-element.452) | copy-start | bytes 3076
  3.8 408.3 %copy-start.23 = (f32[1,256]{1,0:T(1,128)}, f32[1,256]{1,0:T(1,128)S(1)}, u32[]{:S(2)}) copy-start(f32[1,256]{1,0:T(1,128)S(1)} %get-tuple-element.453) | copy-start | bytes 3076
  11.6 73.4 %collective-permute-start = (f32[70,256]{1,0:T(8,128)S(1)}, f32[70,256]{1,0:T(8,128)S(1)}, u32[]{:S(2)}, u32[]{:S(2)}) collective-permute-start(f32[70,256]{1,0:T(8,128)S(1)} %pad_maximum_fusion.2), channel_id=1, source_target_pairs={{0,1},{1,0},{2,3},{3,2},{4,5},{5,4},{6,7},{7,6},{8,9},{9,8},{10,11... | collective-permute-start | bytes 215048 | tf_op jit(solution)/shard_map/ppermute | solution.py:10
  12.1 278.2 %copy-start.8 = (pred[256]{0:T(512)(128)(4,1)}, pred[256]{0:T(512)(128)(4,1)S(1)}, u32[]{:S(2)}) copy-start(pred[256]{0:T(512)(128)(4,1)S(1)} %compare_and_fusion.3) | copy-start | bytes 772
  12.1 288.7 %copy-start.6 = (pred[256]{0:T(512)(128)(4,1)}, pred[256]{0:T(512)(128)(4,1)S(1)}, u32[]{:S(2)}) copy-start(pred[256]{0:T(512)(128)(4,1)S(1)} %compare_and_fusion.2) | copy-start | bytes 772
  90.7 5.5 collective-permute-start.1
  101.9 4.4 collective-permute-start.2
  112.1 5.3 collective-permute-start.3
  217.1 72.1 %collective-permute-start.4 = (f32[70,256]{1,0:T(8,128)S(1)}, f32[70,256]{1,0:T(8,128)S(1)}, u32[]{:S(2)}, u32[]{:S(2)}) collective-permute-start(f32[70,256]{1,0:T(8,128)S(1)} %pad_maximum_fusion.1), channel_id=1, source_target_pairs={{0,1},{1,0},{2,3},{3,2},{4,5},{5,4},{6,7},{7,6},{8,9},{9,8},{10,11... | collective-permute-start | bytes 215048 | tf_op jit(solution)/shard_map/ppermute | solution.py:10
  295.0 4.7 collective-permute-start.5
  305.5 4.4 collective-permute-start.6
  315.7 5.3 collective-permute-start.7
  419.0 72.7 %collective-permute-start.8 = (f32[70,256]{1,0:T(8,128)S(1)}, f32[70,256]{1,0:T(8,128)S(1)}, u32[]{:S(2)}, u32[]{:S(2)}) collective-permute-start(f32[70,256]{1,0:T(8,128)S(1)} %pad_maximum_fusion), channel_id=1, source_target_pairs={{0,1},{1,0},{2,3},{3,2},{4,5},{5,4},{6,7},{7,6},{8,9},{9,8},{10,11... | collective-permute-start | bytes 215048 | tf_op jit(solution)/shard_map/ppermute | solution.py:10
  497.4 5.8 copy-start.7
  497.5 4.7 collective-permute-start.9
  508.1 4.4 collective-permute-start.10
  518.3 5.3 collective-permute-start.11
  553.0 5.0 copy-start.14
  553.0 5.0 copy-start.16
  553.0 5.0 copy-start.18
  553.0 5.0 copy-start.20
  553.0 5.0 copy-start.22
  553.0 5.0 copy-start.24
  553.0 5.0 copy-start.25
  562.4 37.8 %copy-start.51 = (f32[64]{0:T(128)S(1)}, f32[64]{0:T(128)}, u32[]{:S(2)}) copy-start(f32[64]{0:T(128)} %copy-done.50) | copy-start | bytes 772
  562.4 37.8 %copy-start.12 = (f32[64]{0:T(128)S(1)}, f32[64]{0:T(128)}, u32[]{:S(2)}) copy-start(f32[64]{0:T(128)} %copy-done.11) | copy-start | bytes 772
  (32 other events, 133.7 us)
